TPU v7x, 256 devices: a whole 4x4x8 slice. The times are simulated.
256 devices in a mesh: dp: 32 (over x, y, core), mp: 8 (over z).
Axes of the slice: x: 4, y: 4, z: 8, core: 2. Of those that a mesh axis runs over, the one named last changes fastest.
Arguments:
- features: bfloat16 [65536, 2, 512], P('dp'), may hold values from -27 to 27
- projection: bfloat16 [512, 256], replicated, may hold values from -1 to 1
- prototypes: float32 [3000, 256], P('mp'), may hold values from -7 to 7
Outputs:
- grad_prototypes: float32 [3000, 256], P('mp')
- grad_projection: float32 [512, 256], replicated
- loss: float32 [], replicated
All inputs are finite; a program needn't handle non-finite values.
Results may differ from a plain program's by a relative error of at most 0.0019.
The roundings to bfloat16 on the way count: a program that leaves them out, or rounds other values in their place, can miss the bound.
Values may be sent and summed in bfloat16 or wider, within the bound.
A program may use at most 128 MiB of HBM per device.

v0:
```python
import jax
import jax.numpy as jnp
from jax import lax
from jax.sharding import PartitionSpec as P

ITERS = 3
EPSILON_CODES = 0.05
SOFTMAX_TEMPER = 0.1
LOSS_FACTOR = 4096.0
TINY = 1e-06


def unit_rows(values):
    inverse = lax.rsqrt(jnp.sum(values * values, axis=-1, keepdims=True) + TINY)
    return (values * inverse, inverse)


def prototype_totals(values):
    return lax.psum(jnp.sum(values, axis=0), "dp")


def code_totals(values):
    return lax.psum(jnp.sum(values, axis=-1), "mp")


def loss_pieces(
    prototype_logits, softmax_exponent, softmax_denominator, assignments, gradient_factor
):
    swapped_targets = assignments[:, ::-1]
    grad_half = (
        (softmax_exponent / softmax_denominator[..., None] - swapped_targets) * gradient_factor
    ).astype(jnp.bfloat16)
    loss_portion = jnp.sum(
        swapped_targets
        * (prototype_logits * (1.0 / SOFTMAX_TEMPER) - jnp.log(softmax_denominator)[..., None])
    )
    return (grad_half, loss_portion)


def embed_backward(grad_unit, embed_unit, embed_inverse, own_feats):
    along_unit = jnp.sum(embed_unit * grad_unit, axis=-1, keepdims=True)
    grad_raw = ((grad_unit - embed_unit * along_unit) * embed_inverse).astype(jnp.bfloat16)
    return jnp.einsum("bve,bvp->ep", own_feats, grad_raw, preferred_element_type=jnp.float32)


def body(features, projection, prototypes):
    local_rows = features.shape[0]
    own_count = local_rows // lax.axis_size("mp")
    batch_row_count = local_rows * lax.axis_size("dp")
    gradient_factor = LOSS_FACTOR / (2.0 * batch_row_count * SOFTMAX_TEMPER)
    proto_unit, proto_inverse = unit_rows(prototypes)
    proto_half = proto_unit.astype(jnp.bfloat16)
    first_row = lax.axis_index("mp") * own_count
    own_feats = lax.dynamic_slice_in_dim(features, first_row, own_count, 0)
    raw_embed = jnp.einsum("bve,ep->bvp", own_feats, projection, preferred_element_type=jnp.float32)
    embed_unit, embed_inverse = unit_rows(raw_embed)
    embed_half = embed_unit.astype(jnp.bfloat16)
    all_embed = lax.all_gather(embed_half, "mp", axis=0, tiled=True)
    prototype_logits = jnp.einsum(
        "bvp,kp->bvk", all_embed, proto_half, preferred_element_type=jnp.float32
    )
    transport = jnp.exp(prototype_logits * (1.0 / EPSILON_CODES))
    softmax_exponent = jnp.exp(prototype_logits * (1.0 / SOFTMAX_TEMPER))
    soft_part = jnp.sum(softmax_exponent, axis=-1)
    for iteration in range(ITERS - 1):
        transport = transport / prototype_totals(transport)[None]
        transport = transport / code_totals(transport)[..., None]
    transport = transport / prototype_totals(transport)[None]
    softmax_denominator = lax.psum(soft_part, "mp")
    row_sums = code_totals(transport)
    assignments = transport / row_sums[..., None]
    grad_half, loss_portion = loss_pieces(
        prototype_logits, softmax_exponent, softmax_denominator, assignments, gradient_factor
    )
    proto_grad = jnp.einsum("bvk,bvp->kp", grad_half, all_embed, preferred_element_type=jnp.float32)
    proto_grad = lax.psum(proto_grad, "dp")
    grad_unit = lax.psum_scatter(
        jnp.einsum("bvk,kp->bvp", grad_half, proto_half, preferred_element_type=jnp.float32),
        "mp",
        scatter_dimension=0,
        tiled=True,
    )
    weight_part = embed_backward(grad_unit, embed_unit, embed_inverse, own_feats)
    weight_grad, loss_total = lax.psum((weight_part, loss_portion), ("dp", "mp"))
    along_proto = jnp.sum(proto_unit * proto_grad, axis=-1, keepdims=True)
    grad_protos = (proto_grad - proto_unit * along_proto) * proto_inverse
    loss_value = -loss_total / (2.0 * batch_row_count)
    return (grad_protos, weight_grad, loss_value)


def solution(mesh):
    return jax.shard_map(
        body,
        mesh=mesh,
        in_specs=(P("dp", None, None), P(), P("mp", None)),
        out_specs=(P("mp", None), P(), P()),
        check_vma=False,
    )
```

profile of v0, /device:TPU:2, one launch (start us, length us, event | category | flops | bytes accessed | tf_op | source)
XLA Modules:
  0.0 803.6 jit_solution(7048572155357733132)
XLA Ops:
  7.2 0.0 copy-start
  7.2 0.0 all-gather.2.cloned.1.call-start
  7.2 1.4 constant_dynamic-slice_fusion
  8.7 0.0 copy-start.3
  8.7 0.8 copy-done.3
  9.5 0.0 copy-done
  9.5 0.4 multiply_reduce_fusion.1
  9.9 0.7 multiply_convert_fusion.1
  10.6 0.0 all-gather.2.cloned.1.call-update
  10.6 0.0 reduce-scatter.2.cloned.1.call-start
  10.7 1.1 multiply_reduce_fusion.4
  11.8 49.1 %all-gather.2.cloned.1.call-done = bf16[2048,2,256]{0,2,1:T(8,128)(2,1)} async-done(((bf16[256,2,256]{0,2,1:T(8,128)(2,1)}), bf16[2048,2,256]{0,2,1:T(8,128)(2,1)}) %all-gather.2.cloned.1.call-update) | async-done | bytes 2097168 | tf_op jit(solution)/shard_map/all_gather | solution.py:58
  60.9 5.4 fusion.12
  66.3 53.0 %psum.71 = f32[2,375]{1,0:T(2,128)S(1)} all-reduce(f32[2,375]{1,0:T(2,128)S(1)} %get-tuple-element.11), channel_id=1, replica_groups=mesh['dp'=32,'mp'=8] {'dp'}, use_global_device_ids=true, to_apply=%region_5.0 | all-reduce | flops 750 | bytes 6000 | tf_op jit(solution)/shard_map/psum | solution.py:19
  119.3 3.8 exponential_reduce_fusion
  123.2 29.9 %psum.72 = f32[2048,2]{0,1:T(2,128)S(1)} all-reduce(f32[2048,2]{0,1:T(2,128)S(1)} %get-tuple-element.4), channel_id=1, replica_groups=mesh['dp'=32,'mp'=8] {'mp'}, use_global_device_ids=true, to_apply=%region_7.0 | all-reduce | flops 4096 | bytes 32768 | tf_op jit(solution)/shard_map/psum | solution.py:23
  153.0 4.4 fusion.8
  157.5 54.7 %psum.73 = f32[2,375]{1,0:T(2,128)S(1)} all-reduce(f32[2,375]{1,0:T(2,128)S(1)} %fusion.8), channel_id=1, replica_groups=mesh['dp'=32,'mp'=8] {'dp'}, use_global_device_ids=true, to_apply=%region_9.0 | all-reduce | flops 750 | bytes 6000 | tf_op jit(solution)/shard_map/psum | solution.py:19
  212.1 3.7 fusion.9
  215.9 27.0 %psum.74 = f32[2048,2]{0,1:T(2,128)S(1)} all-reduce(f32[2048,2]{0,1:T(2,128)S(1)} %fusion.9), channel_id=1, replica_groups=mesh['dp'=32,'mp'=8] {'mp'}, use_global_device_ids=true, to_apply=%region_11.0 | all-reduce | flops 4096 | bytes 32768 | tf_op jit(solution)/shard_map/psum | solution.py:23
  242.9 3.9 fusion.10
  246.8 62.7 %psum.75 = f32[2,375]{1,0:T(2,128)S(1)} all-reduce(f32[2,375]{1,0:T(2,128)S(1)} %fusion.10), channel_id=1, replica_groups=mesh['dp'=32,'mp'=8] {'dp'}, use_global_device_ids=true, to_apply=%region_13.0 | all-reduce | flops 750 | bytes 6000 | tf_op jit(solution)/shard_map/psum | solution.py:19
  309.5 4.3 fusion.11
  313.8 27.7 %all-reduce = (f32[2048,2]{0,1:T(2,128)S(1)}, f32[2048,2]{0,1:T(2,128)S(1)}) all-reduce(f32[2048,2]{0,1:T(2,128)S(1)} %fusion.11, f32[2048,2]{0,1:T(2,128)S(1)} %get-tuple-element.3), channel_id=1, replica_groups=mesh['dp'=32,'mp'=8] {'mp'}, use_global_device_ids=true, to_apply=%region_15.0 | all-reduce | flops 8192 | bytes 65536 | tf_op jit(solution)/shard_map/psum | solution.py:23
  341.5 0.0 slice-start.1
  341.5 5.1 fusion.7
  346.6 0.0 slice-done
  346.6 0.0 slice-done.1
  346.7 0.0 copy-start.2
  346.7 2.6 multiply_reduce_fusion
  349.2 1.6 copy-done.1
  350.9 0.0 copy-done.2
  350.9 3.3 fusion.28
  354.2 0.0 reduce-scatter.2.cloned.1.call-update
  354.2 0.0 all-reduce.4.cloned.1.call-start
  354.3 4.3 convolution_bitcast_fusion.1
  358.6 0.0 all-reduce.4.cloned.1.call-update
  358.7 0.0 all-reduce.6.cloned.1.call-start
  358.7 90.6 %psum.79 = f32[]{:T(128)} all-reduce(f32[]{:T(128)} %get-tuple-element.7), channel_id=1, replica_groups=mesh['dp'=32,'mp'=8] {'dp','mp'}, use_global_device_ids=true, to_apply=%region_22.0 | all-reduce | flops 1 | bytes 8 | tf_op jit(solution)/shard_map/psum | solution.py:84
  449.9 0.0 reduce-scatter.2.cloned.1.call-done
  450.0 0.0 copy-done.4
  450.0 2.5 convolution_bitcast_fusion
  452.5 0.0 all-reduce.6.cloned.1.call-update
  452.5 83.7 %all-reduce.4.cloned.1.call-done = f32[375,256]{1,0:T(8,128)} async-done(((f32[375,256]{1,0:T(8,128)}), f32[375,256]{1,0:T(8,128)}) %all-reduce.4.cloned.1.call-update) | async-done | bytes 384016 | tf_op jit(solution)/shard_map/psum | solution.py:76
  536.2 1.2 multiply_reduce_fusion.3
  537.4 1.9 subtract_multiply_fusion
  539.3 254.8 %all-reduce.6.cloned.1.call-done = f32[512,256]{1,0:T(8,128)} async-done(((f32[512,256]{1,0:T(8,128)}), f32[512,256]{1,0:T(8,128)}) %all-reduce.6.cloned.1.call-update) | async-done | bytes 524304 | tf_op jit(solution)/shard_map/psum | solution.py:84
  794.1 1.9 copy.29
  (7 shorter events, 0.0 us)
Async XLA Ops:
  7.2 2.3 copy-start
  7.2 53.7 %all-gather.2.cloned.1.call-start = ((), (), s32[]{:S(2)}) async-start(), calls=%async_computation.1 | async-start | bytes 2359296 | tf_op jit(solution)/shard_map/all_gather | solution.py:58
  8.7 0.8 copy-start.3
  10.6 439.3 %reduce-scatter.2.cloned.1.call-start = ((), (), s32[]{:S(2)}) async-start(), calls=%async_computation.3 | async-start | bytes 4718592 | tf_op jit(solution)/shard_map/reduce_scatter | solution.py:77
  309.5 37.1 %slice-start = ((s8[6160384]{0:T(1024)(128)(4,1)}), s8[1966080]{0:T(1024)(128)(4,1)S(1)}, s32[]{:S(2)}) async-start(s8[6160384]{0:T(1024)(128)(4,1)} %bitcast.19), calls=%async_computation.5 | async-start | bytes 3932160
  341.5 5.1 slice-start.1
  346.7 4.2 copy-start.2
  349.2 1.6 copy-start.1
  354.2 95.8 %copy-start.4 = (bf16[256,2,512]{2,1,0:T(2,128)(2,1)S(1)}, bf16[256,2,512]{2,1,0:T(2,128)(2,1)}, u32[]{:S(2)}) copy-start(bf16[256,2,512]{2,1,0:T(2,128)(2,1)} %copy-done.3) | copy-start | bytes 1572868
  354.2 181.9 %all-reduce.4.cloned.1.call-start = ((), (), s32[]{:S(2)}) async-start(), calls=%async_computation.2 | async-start | bytes 770048 | tf_op jit(solution)/shard_map/psum | solution.py:76
  358.7 435.4 %all-reduce.6.cloned.1.call-start = ((), (), s32[]{:S(2)}) async-start(), calls=%async_computation.4 | async-start | bytes 1048576 | tf_op jit(solution)/shard_map/psum | solution.py:84
Sparse Core Ops, SparseCore 0:
  10.7 50.1 all-gather.1
  354.4 66.9 reduce-scatter.1
  425.2 110.8 all-reduce.3
  542.1 251.9 all-reduce.5
where the time goes:
time: 804 us
  waiting for transfers between devices  388 us (48%)
  blocking collectives  345 us (43%)
  other arithmetic  32.9 us (4%)
  matrix products  16 us (2%)
  between operations  15.7 us (2%)
    psum x1, waiting for transfers between devices, body(): lax.psum((weight_part, loss_portion), ('dp', 'mp'))  255 us
    psum x3, blocking collectives, prototype_totals(): return lax.psum(jnp.sum(values, axis=0), 'dp')  170 us
    psum x1, blocking collectives, body(): lax.psum((weight_part, loss_portion), ('dp', 'mp'))  90.6 us
    psum x3, blocking collectives, code_totals(): return lax.psum(jnp.sum(values, axis=-1), 'mp')  84.6 us
    psum x1, waiting for transfers between devices, body(): proto_grad = lax.psum(proto_grad, 'dp')  83.7 us
    all_gather x1, waiting for transfers between devices, body(): all_embed = lax.all_gather(embed_half, 'mp', axis=0, tiled=True)  49.1 us
  transfers between devices with their start and end apart: 4, of which 3 were waited for; matrix products, arithmetic and copies ran while one was open for 1% of the time, Pallas kernels for 0%

commit v1 on v0

--- a/solution.py
+++ b/solution.py
@@ -1,3 +1,4 @@
+import functools
 import jax
 import jax.numpy as jnp
 from jax import lax
@@ -8,6 +9,15 @@
 SOFTMAX_TEMPER = 0.1
 LOSS_FACTOR = 4096.0
 TINY = 1e-06
+
+
+def balance_ratios(a0, net_axis, named_axis):
+    work_now = jax.lax.psum(a0, axis_name=net_axis)
+    x_now = jax.lax.psum(work_now, axis_name=named_axis)
+    return x_now
+
+
+_hold_pools = functools.partial(balance_ratios, net_axis="mp", named_axis="dp")
 
 
 def unit_rows(values):
@@ -81,7 +91,7 @@
         tiled=True,
     )
     weight_part = embed_backward(grad_unit, embed_unit, embed_inverse, own_feats)
-    weight_grad, loss_total = lax.psum((weight_part, loss_portion), ("dp", "mp"))
+    weight_grad, loss_total = _hold_pools((weight_part, loss_portion))
     along_proto = jnp.sum(proto_unit * proto_grad, axis=-1, keepdims=True)
     grad_protos = (proto_grad - proto_unit * along_proto) * proto_inverse
     loss_value = -loss_total / (2.0 * batch_row_count)

time: 804 us -> 628 us (0.78)
  waiting for transfers between devices: 388 us -> 229 us
  blocking collectives: 345 us -> 326 us
    psum x1, waiting for transfers between devices: 255 us -> 68.8 us  [balance_ratios(): work_now = jax.lax.psum(a0, axis_name=net_axis)]
    reduce_scatter x1, waiting for transfers between devices: 0.02 us -> 66.1 us  [body(): lax.psum_scatter(jnp.einsum('bvk,kp->bvp', grad_half, proto_half, preferr...]
    psum x1, waiting for transfers between devices: 83.7 us -> 45.1 us  [body(): proto_grad = lax.psum(proto_grad, 'dp')]
    psum x1 -> x2, blocking collectives: 90.6 us -> 70.7 us  [the longest x1 53.6 us: balance_ratios(): x_now = jax.lax.psum(work_now, axis_name=named_axis)]
  transfers between devices with their start and end apart: 4 -> 4, of which waited for: 3 -> 4; matrix products, arithmetic and copies ran while one was open for 1% -> 1% of each run, Pallas kernels for 0% -> 0%
where the time goes in v1:
time: 628 us; the launch traced here: 626 us
  blocking collectives  326 us (52%)
  waiting for transfers between devices  229 us (36%)
  other arithmetic  33.2 us (5%)
  between operations  15.7 us (2%)
  matrix products  15.4 us (2%)
  local copies, waits for them, and re-layouts  6.56 us (1%)
    psum x3, blocking collectives, prototype_totals(): return lax.psum(jnp.sum(values, axis=0), 'dp')  170 us
    psum x3, blocking collectives, code_totals(): return lax.psum(jnp.sum(values, axis=-1), 'mp')  84.6 us
    psum x1, waiting for transfers between devices, balance_ratios(): work_now = jax.lax.psum(a0, axis_name=net_axis)  68.8 us
    reduce_scatter x1, waiting for transfers between devices, body(): lax.psum_scatter(jnp.einsum('bvk,kp->bvp', grad_half, proto_half, preferr...  66.1 us
    psum x1, blocking collectives, balance_ratios(): x_now = jax.lax.psum(work_now, axis_name=named_axis)  53.6 us
    all_gather x1, waiting for transfers between devices, body(): all_embed = lax.all_gather(embed_half, 'mp', axis=0, tiled=True)  49.1 us
    psum x1, waiting for transfers between devices, body(): proto_grad = lax.psum(proto_grad, 'dp')  45.1 us
    psum x1, blocking collectives, balance_ratios(): work_now = jax.lax.psum(a0, axis_name=net_axis)  17 us
  transfers between devices with their start and end apart: 4, of which 4 were waited for; matrix products, arithmetic and copies ran while one was open for 1% of the time, Pallas kernels for 0%

profile of v1, /device:TPU:2, one launch (start us, length us, event | category | flops | bytes accessed | tf_op | source)
XLA Modules:
  0.0 625.8 jit_solution(4891146653210776559)
XLA Ops:
  7.2 0.0 copy-start
  7.2 0.0 all-gather.2.cloned.1.call-start
  7.2 1.4 constant_dynamic-slice_fusion
  8.7 0.0 copy-start.5
  8.7 0.8 copy-done.5
  9.5 0.0 copy-done
  9.5 0.4 multiply_reduce_fusion.1
  9.8 0.0 copy-start.4
  9.9 0.8 copy-done.4
  10.6 0.7 multiply_convert_fusion.1
  11.4 0.0 all-gather.2.cloned.1.call-update
  11.4 0.0 reduce-scatter.2.cloned.1.call-start
  11.5 1.1 multiply_reduce_fusion.4
  12.6 49.1 %all-gather.2.cloned.1.call-done = bf16[2048,2,256]{0,2,1:T(8,128)(2,1)} async-done(((bf16[256,2,256]{0,2,1:T(8,128)(2,1)}), bf16[2048,2,256]{0,2,1:T(8,128)(2,1)}) %all-gather.2.cloned.1.call-update) | async-done | bytes 2097168 | tf_op jit(solution)/shard_map/all_gather | solution.py:68
  61.7 5.4 fusion.12
  67.1 53.0 %psum.85 = f32[2,375]{1,0:T(2,128)S(1)} all-reduce(f32[2,375]{1,0:T(2,128)S(1)} %get-tuple-element.13), channel_id=1, replica_groups=mesh['dp'=32,'mp'=8] {'dp'}, use_global_device_ids=true, to_apply=%region_5.0 | all-reduce | flops 750 | bytes 6000 | tf_op jit(solution)/shard_map/psum | solution.py:29
  120.1 3.8 exponential_reduce_fusion
  123.9 29.9 %psum.86 = f32[2048,2]{0,1:T(2,128)S(1)} all-reduce(f32[2048,2]{0,1:T(2,128)S(1)} %get-tuple-element.4), channel_id=1, replica_groups=mesh['dp'=32,'mp'=8] {'mp'}, use_global_device_ids=true, to_apply=%region_7.0 | all-reduce | flops 4096 | bytes 32768 | tf_op jit(solution)/shard_map/psum | solution.py:33
  153.8 4.4 fusion.8
  158.2 54.7 %psum.87 = f32[2,375]{1,0:T(2,128)S(1)} all-reduce(f32[2,375]{1,0:T(2,128)S(1)} %fusion.8), channel_id=1, replica_groups=mesh['dp'=32,'mp'=8] {'dp'}, use_global_device_ids=true, to_apply=%region_9.0 | all-reduce | flops 750 | bytes 6000 | tf_op jit(solution)/shard_map/psum | solution.py:29
  212.9 3.7 fusion.9
  216.7 27.0 %psum.88 = f32[2048,2]{0,1:T(2,128)S(1)} all-reduce(f32[2048,2]{0,1:T(2,128)S(1)} %fusion.9), channel_id=1, replica_groups=mesh['dp'=32,'mp'=8] {'mp'}, use_global_device_ids=true, to_apply=%region_11.0 | all-reduce | flops 4096 | bytes 32768 | tf_op jit(solution)/shard_map/psum | solution.py:33
  243.7 3.9 fusion.10
  247.6 62.7 %psum.89 = f32[2,375]{1,0:T(2,128)S(1)} all-reduce(f32[2,375]{1,0:T(2,128)S(1)} %fusion.10), channel_id=1, replica_groups=mesh['dp'=32,'mp'=8] {'dp'}, use_global_device_ids=true, to_apply=%region_13.0 | all-reduce | flops 750 | bytes 6000 | tf_op jit(solution)/shard_map/psum | solution.py:29
  310.3 4.3 fusion.11
  314.6 27.7 %all-reduce.1 = (f32[2048,2]{0,1:T(2,128)S(1)}, f32[2048,2]{0,1:T(2,128)S(1)}) all-reduce(f32[2048,2]{0,1:T(2,128)S(1)} %fusion.11, f32[2048,2]{0,1:T(2,128)S(1)} %get-tuple-element.3), channel_id=1, replica_groups=mesh['dp'=32,'mp'=8] {'mp'}, use_global_device_ids=true, to_apply=%region_15.0 | all-reduce | flops 8192 | bytes 65536 | tf_op jit(solution)/shard_map/psum | solution.py:33
  342.3 0.0 slice-start.1
  342.3 5.1 fusion.7
  347.4 0.0 copy-start.3
  347.5 2.6 multiply_reduce_fusion
  350.0 1.6 copy-done.1
  351.7 0.0 copy-done.3
  351.7 3.3 fusion.28
  355.0 0.0 reduce-scatter.2.cloned.1.call-update
  355.1 0.0 all-reduce.5.cloned.1.call-start
  355.1 66.1 %reduce-scatter.2.cloned.1.call-done = f32[256,2,256]{0,2,1:T(8,128)} async-done(((f32[2048,2,256]{0,2,1:T(8,128)}), f32[256,2,256]{0,2,1:T(8,128)}) %reduce-scatter.2.cloned.1.call-update) | async-done | bytes 524304 | tf_op jit(solution)/shard_map/reduce_scatter | solution.py:87
  421.2 3.0 convolution_bitcast_fusion
  424.2 0.0 all-reduce.5.cloned.1.call-update
  424.2 0.0 all-reduce.7.cloned.1.call-start
  424.3 3.4 convolution_bitcast_fusion.1
  427.6 68.8 %all-reduce.5.cloned.1.call-done = f32[512,256]{1,0:T(8,128)} async-done(((f32[512,256]{1,0:T(8,128)}), f32[512,256]{1,0:T(8,128)}) %all-reduce.5.cloned.1.call-update) | async-done | bytes 524304 | tf_op jit(solution)/shard_map/psum | solution.py:15
  496.4 0.0 all-reduce.7.cloned.1.call-update
  496.5 17.0 %psum.94 = f32[]{:T(128)} all-reduce(f32[]{:T(128)} %get-tuple-element.9), channel_id=1, replica_groups=mesh['dp'=32,'mp'=8] {'mp'}, use_global_device_ids=true, to_apply=%region_23.0 | all-reduce | flops 1 | bytes 8 | tf_op jit(solution)/shard_map/psum | solution.py:15
  513.5 53.6 %psum.95 = f32[]{:T(128)} all-reduce(f32[]{:T(128)} %psum.94), channel_id=1, replica_groups=mesh['dp'=32,'mp'=8] {'dp'}, use_global_device_ids=true, to_apply=%region_24.0 | all-reduce | flops 1 | bytes 8 | tf_op jit(solution)/shard_map/psum | solution.py:16
  567.8 45.1 %all-reduce.7.cloned.1.call-done = (f32[375,256]{1,0:T(8,128)}, f32[512,256]{1,0:T(8,128)}) async-done(((f32[375,256]{1,0:T(8,128)}, f32[512,256]{1,0:T(8,128)}), (f32[375,256]{1,0:T(8,128)}, f32[512,256]{1,0:T(8,128)})) %all-reduce.7.cloned.1.call-update) | async-done | bytes 908304 | tf_op jit(solution)/shard_map/psum | solution.py:86
  612.9 1.3 multiply_reduce_fusion.3
  614.2 2.0 subtract_multiply_fusion
  616.2 1.9 copy.30
  (10 shorter events, 0.0 us)
Async XLA Ops:
  7.2 2.3 copy-start
  7.2 54.5 %all-gather.2.cloned.1.call-start = ((), (), s32[]{:S(2)}) async-start(), calls=%async_computation.1 | async-start | bytes 2359296 | tf_op jit(solution)/shard_map/all_gather | solution.py:68
  8.7 0.8 copy-start.5
  9.8 0.8 copy-start.4
  11.4 409.8 %reduce-scatter.2.cloned.1.call-start = ((), (), s32[]{:S(2)}) async-start(), calls=%async_computation.2 | async-start | bytes 4718592 | tf_op jit(solution)/shard_map/reduce_scatter | solution.py:87
  310.3 37.1 %slice-start = ((s8[6160384]{0:T(1024)(128)(4,1)}), s8[1966080]{0:T(1024)(128)(4,1)S(1)}, s32[]{:S(2)}) async-start(s8[6160384]{0:T(1024)(128)(4,1)} %bitcast.19), calls=%async_computation.5 | async-start | bytes 3932160
  342.3 5.1 slice-start.1
  347.4 4.2 copy-start.3
  350.0 1.6 copy-start.1
  355.0 69.2 %copy-start.2 = (bf16[2048,2,375]{0,2,1:T(8,128)(2,1)S(1)}, bf16[2048,2,375]{0,2,1:T(8,128)(2,1)}, u32[]{:S(2)}) copy-start(bf16[2048,2,375]{0,2,1:T(8,128)(2,1)} %copy-done.1) | copy-start | bytes 9216004
  355.1 141.4 %all-reduce.5.cloned.1.call-start = ((), (), s32[]{:S(2)}) async-start(), calls=%async_computation.3 | async-start | bytes 1048576 | tf_op jit(solution)/shard_map/psum | solution.py:15
  424.2 188.7 %all-reduce.7.cloned.1.call-start = ((), (), s32[]{:S(2)}) async-start(), calls=%async_computation.4 | async-start | bytes 1818624 | tf_op jit(solution)/shard_map/psum | solution.py:86
Sparse Core Ops, SparseCore 0:
  11.5 50.1 all-gather.1
  355.2 66.0 reduce-scatter.1
  424.3 72.0 all-reduce.4
  500.6 112.1 all-reduce.6
